TPU v7x, 32 devices: a whole 2x2x4 slice. The times are simulated.
32 devices in a mesh: outer: 1, inner: 32 (over z, y, x, core).
Axes of the slice: x: 2, y: 2, z: 4, core: 2. Of those that a mesh axis runs over, the one named last changes fastest.
Arguments:
- b_leaf: float32 [8192, 64], P(('outer', 'inner')), may hold values from -6 to 6
- b_sep: float32 [256, 64], P(('outer', 'inner')), may hold values from -6 to 6
- b_root: float32 [256, 64], P(('outer', 'inner')), may hold values from -6 to 6
- leaf_linv: float32 [8192, 256], P(('outer', 'inner')), as said below
- leaf_uinv: float32 [8192, 256], P(('outer', 'inner')), as said below
- leaf_lower: float32 [8192, 256], P(('outer', 'inner')), as said below
- leaf_upper: float32 [8192, 256], P(('outer', 'inner')), as said below
- sep_rows: int32 [32, 256], P(('outer', 'inner')), may hold values from 0 to 255, as said below
- sep_linv: float32 [256, 256], P(('outer', 'inner')), as said below
- sep_uinv: float32 [256, 256], P(('outer', 'inner')), as said below
- sep_lower: float32 [256, 256], P(None, ('outer', 'inner')), as said below
- sep_upper: float32 [256, 256], P(('outer', 'inner')), as said below
- root_linv: float32 [256, 256], P(('outer', 'inner')), as said below
- root_uinv: float32 [256, 256], P(('outer', 'inner')), as said below
- basis_leaf: float32 [8192, 512], P(('outer', 'inner')), as said below
- basis_sep: float32 [256, 512], P(('outer', 'inner')), as said below
- basis_root: float32 [256, 512], P(('outer', 'inner')), as said below
- g_blocks: float32 [32768, 128], P(('outer', 'inner')), may hold values from -0.25 to 0.25
- c_blocks: float32 [32768, 128], P(('outer', 'inner')), may hold values from -0.25 to 0.25
- block_cols: int32 [64, 4], P(('outer', 'inner')), may hold values from 0 to 1
Outputs:
- v_leaf: float32 [8192, 64], P(('outer', 'inner'))
- v_sep: float32 [256, 64], P(('outer', 'inner'))
- v_root: float32 [256, 64], P(('outer', 'inner'))
- coefficients: float32 [512, 64], replicated
- reduced_g: float32 [64, 64], replicated
- reduced_c: float32 [64, 64], replicated
Inputs may be any that keep to these rules, and one draw needn't show every extreme that they name: `sep_rows`: each row holds 256 distinct numbers; every row names 0 and 255. `leaf_linv`: lower triangular in each diagonal block of the stack, nonzero diagonal. `leaf_uinv`: upper triangular in each diagonal block of the stack, nonzero diagonal. `sep_linv`: lower triangular in each block of 256 rows, nonzero diagonal. `sep_uinv`: upper triangular in each block of 256 rows, nonzero diagonal. `root_linv`: lower triangular, nonzero diagonal. `root_uinv`: upper triangular, nonzero diagonal. `leaf_lower`: entries of order one over the square root of 256. `leaf_upper`: entries of order one over the square root of 256. `sep_lower`: entries of order one over the square root of the number of its columns. `sep_upper`: entries of order one over the square root of 256. basis_leaf, basis_sep and basis_root stacked by rows form Q with Q^T Q = 8704 I up to float32 rounding. `basis_sep`: part of the stacked Q described with basis_leaf. `basis_root`: part of the stacked Q described with basis_leaf.
All inputs are finite; a program needn't handle non-finite values.
Results may differ from a plain program's by a relative error of at most 0.0003.
Values sent between devices are 32-bit elements; how exact they have to be, the bound alone decides.
No kernel may reach another device: no remote copies, remote signals or barrier semaphores. Data moves between devices by JAX's collectives and lax.ppermute only.
A program may use at most 64 MiB of HBM per device.

v0:
```python
import jax
import jax.numpy as jnp
from jax import lax
from jax.sharding import PartitionSpec as P


def matmul_exact(left, right):
    return jnp.dot(left, right, precision=lax.Precision.HIGHEST, preferred_element_type=jnp.float32)


def contract_rows(left, right):
    return lax.dot_general(
        left,
        right,
        (((0,), (0,)), ((), ())),
        precision=lax.Precision.HIGHEST,
        preferred_element_type=jnp.float32,
    )


def shards(
    b_leaf,
    b_sep,
    b_root,
    leaf_linv,
    leaf_uinv,
    leaf_lower,
    leaf_upper,
    sep_rows,
    sep_linv,
    sep_uinv,
    sep_lower,
    sep_upper,
    root_linv,
    root_uinv,
    basis_leaf,
    basis_sep,
    basis_root,
    g_blocks,
    c_blocks,
    block_cols,
):
    ports = b_leaf.shape[1]
    sep_local = b_sep.shape[0]
    root_local = b_root.shape[0]
    sep_width = sep_linv.shape[1]
    selector = (sep_rows[0][:, None] == jnp.arange(sep_width, dtype=jnp.int32)[None, :]).astype(
        jnp.float32
    )
    y_leaf = matmul_exact(leaf_linv, b_leaf)
    contrib = matmul_exact(leaf_lower, y_leaf)
    t_sep = lax.psum_scatter(
        contract_rows(selector, contrib), "inner", scatter_dimension=0, tiled=True
    )
    sep_whole = lax.all_gather(b_sep - t_sep, "inner", axis=0, tiled=True)
    y_sep = matmul_exact(sep_linv, sep_whole)
    summed = lax.psum(matmul_exact(sep_lower, y_sep), ("outer", "inner"))
    sources = lax.all_gather(b_root, ("outer", "inner"), axis=0, tiled=True)
    y_root = matmul_exact(root_linv, sources - summed)
    y_root_all = lax.all_gather(y_root, ("outer", "inner"), axis=0, tiled=True)
    x_root = matmul_exact(root_uinv, y_root_all)
    x_root_all = lax.all_gather(x_root, ("outer", "inner"), axis=0, tiled=True)
    z_sep = y_sep - matmul_exact(sep_upper, x_root_all)
    z_sep_all = lax.all_gather(z_sep, "inner", axis=0, tiled=True)
    x_sep = matmul_exact(sep_uinv, z_sep_all)
    x_sep_all = lax.all_gather(x_sep, "inner", axis=0, tiled=True)
    coupled = matmul_exact(selector, x_sep_all)
    x_leaf = matmul_exact(leaf_uinv, y_leaf - matmul_exact(leaf_upper, coupled))
    node_count = float(
        lax.axis_size("outer") * lax.axis_size("inner") * (b_leaf.shape[0] + sep_local + root_local)
    )
    pieces_x = (x_leaf, x_sep, x_root)
    pieces_q = (basis_leaf, basis_sep, basis_root)
    projected = (
        contract_rows(basis_leaf, x_leaf)
        + contract_rows(basis_sep, x_sep)
        + contract_rows(basis_root, x_root)
    )
    coefficients = lax.psum(projected, ("outer", "inner")) / node_count
    cleaned = [
        values - matmul_exact(basis, coefficients) for basis, values in zip(pieces_q, pieces_x)
    ]
    local_gram = (
        contract_rows(cleaned[0], cleaned[0])
        + contract_rows(cleaned[1], cleaned[1])
        + contract_rows(cleaned[2], cleaned[2])
    )
    gram_matrix = lax.psum(local_gram, ("outer", "inner")) / node_count
    chol_lower = jnp.linalg.cholesky(gram_matrix)
    inverse_lower = lax.linalg.triangular_solve(
        chol_lower, jnp.eye(ports, dtype=jnp.float32), left_side=True, lower=True
    )
    v_leaf = matmul_exact(cleaned[0], inverse_lower.T)
    v_sep = matmul_exact(cleaned[1], inverse_lower.T)
    v_root = matmul_exact(cleaned[2], inverse_lower.T)
    block_rows = block_cols.shape[0]
    stored = block_cols.shape[1]
    block_size = g_blocks.shape[1]
    blocked = v_leaf.reshape(block_rows, block_size, ports)
    picked = blocked[block_cols]
    g_tiles = g_blocks.reshape(block_rows, stored, block_size, block_size)
    c_tiles = c_blocks.reshape(block_rows, stored, block_size, block_size)
    g_image = jnp.einsum("rwij,rwjp->rip", g_tiles, picked, precision=lax.Precision.HIGHEST)
    c_image = jnp.einsum("rwij,rwjp->rip", c_tiles, picked, precision=lax.Precision.HIGHEST)
    g_local = jnp.einsum("rip,riq->pq", blocked, g_image, precision=lax.Precision.HIGHEST)
    c_local = jnp.einsum("rip,riq->pq", blocked, c_image, precision=lax.Precision.HIGHEST)
    g_summed, c_summed = lax.psum((g_local, c_local), ("outer", "inner"))
    return (v_leaf, v_sep, v_root, coefficients, g_summed / node_count, c_summed / node_count)


def solution(mesh):
    return jax.shard_map(
        shards,
        mesh=mesh,
        in_specs=(
            P(("outer", "inner"), None),
            P(("outer", "inner"), None),
            P(("outer", "inner"), None),
            P(("outer", "inner"), None),
            P(("outer", "inner"), None),
            P(("outer", "inner"), None),
            P(("outer", "inner"), None),
            P(("outer", "inner"), None),
            P(("outer", "inner"), None),
            P(("outer", "inner"), None),
            P(None, ("outer", "inner")),
            P(("outer", "inner"), None),
            P(("outer", "inner"), None),
            P(("outer", "inner"), None),
            P(("outer", "inner"), None),
            P(("outer", "inner"), None),
            P(("outer", "inner"), None),
            P(("outer", "inner"), None),
            P(("outer", "inner"), None),
            P(("outer", "inner"), None),
        ),
        out_specs=(
            P(("outer", "inner"), None),
            P(("outer", "inner"), None),
            P(("outer", "inner"), None),
            P(),
            P(),
            P(),
        ),
        check_vma=False,
    )
```

profile of v0, /device:TPU:0, one launch (start us, length us, event | category | flops | bytes accessed | tf_op | source)
XLA Modules:
  0.0 685.7 jit_solution(16916968704119471954)
XLA Ops:
  7.2 1.4 fusion.17
  9.0 0.7 copy-done.16
  9.7 1.0 fusion.8
  10.8 130.4 %all-reduce.10.cloned.1.call-done = f32[256,64]{1,0:T(8,128)} async-done(((f32[256,64]{1,0:T(8,128)}), f32[256,64]{1,0:T(8,128)}) %all-reduce.10.cloned.1.call-update) | async-done | bytes 65552
  141.3 0.7 dynamic-slice_subtract_fusion
  142.0 40.0 %all_gather.18 = f32[256,64]{1,0:T(8,128)S(1)} all-gather(f32[8,64]{1,0:T(8,128)S(1)} %dynamic-slice_subtract_fusion), channel_id=1, replica_groups=mesh['outer'=1,'inner'=32] {'inner'}, dimensions={0}, use_global_device_ids=true | all-gather | bytes 67584 | tf_op jit(solution)/shard_map/all_gather | solution.py:55
  182.7 0.9 convolution_bitcast_fusion.3
  183.7 0.6 copy-done.19
  184.3 37.0 %all_gather.19 = f32[256,64]{1,0:T(8,128)S(1)} all-gather(f32[8,64]{1,0:T(8,128)S(1)} %copy-done.18), channel_id=1, replica_groups=mesh['outer'=1,'inner'=32] {'outer','inner'}, dimensions={0}, use_global_device_ids=true | all-gather | bytes 67584 | tf_op jit(solution)/shard_map/all_gather | solution.py:58
  221.4 77.8 %all-reduce.6.cloned.1.call-done = f32[256,64]{0,1:T(8,128)} async-done(((f32[256,64]{0,1:T(8,128)}), f32[256,64]{0,1:T(8,128)}) %all-reduce.6.cloned.1.call-update) | async-done | bytes 65552 | tf_op jit(solution)/shard_map/psum | solution.py:57
  299.2 1.0 convolution_bitcast_fusion.8
  300.2 40.4 %all_gather.20 = f32[256,64]{1,0:T(8,128)S(1)} all-gather(f32[8,64]{1,0:T(8,128)S(1)} %convolution_bitcast_fusion.8), channel_id=1, replica_groups=mesh['outer'=1,'inner'=32] {'outer','inner'}, dimensions={0}, use_global_device_ids=true | all-gather | bytes 67584 | tf_op jit(solution)/shard_map/all_gather | solution.py:60
  340.8 37.0 %all_gather.21 = f32[256,64]{1,0:T(8,128)S(1)} all-gather(f32[8,64]{1,0:T(8,128)S(1)} %bitcast.119), channel_id=1, replica_groups=mesh['outer'=1,'inner'=32] {'outer','inner'}, dimensions={0}, use_global_device_ids=true | all-gather | bytes 67584 | tf_op jit(solution)/shard_map/all_gather | solution.py:62
  377.9 38.3 %all_gather.22 = f32[256,64]{1,0:T(8,128)S(1)} all-gather(f32[8,64]{1,0:T(8,128)S(1)} %fusion.5), channel_id=1, replica_groups=mesh['outer'=1,'inner'=32] {'inner'}, dimensions={0}, use_global_device_ids=true | all-gather | bytes 67584 | tf_op jit(solution)/shard_map/all_gather | solution.py:64
  416.4 37.0 %all_gather.23 = f32[256,64]{1,0:T(8,128)S(1)} all-gather(f32[8,64]{1,0:T(8,128)S(1)} %bitcast.120), channel_id=1, replica_groups=mesh['outer'=1,'inner'=32] {'inner'}, dimensions={0}, use_global_device_ids=true | all-gather | bytes 67584 | tf_op jit(solution)/shard_map/all_gather | solution.py:66
  455.2 1.1 fusion.1
  456.4 122.1 %all-reduce.8.cloned.1.call-done = f32[512,64]{0,1:T(8,128)} async-done(((f32[512,64]{0,1:T(8,128)}), f32[512,64]{0,1:T(8,128)}) %all-reduce.8.cloned.1.call-update) | async-done | bytes 131088 | tf_op jit(solution)/shard_map/psum | solution.py:79
  578.5 0.9 broadcast_multiply_fusion
  579.4 0.6 convolution_subtract_fusion
  581.2 39.4 %psum.37 = f32[64,64]{0,1:T(8,128)S(1)} all-reduce(f32[64,64]{0,1:T(8,128)S(1)} %convolution_add_fusion.1), channel_id=1, replica_groups=mesh['outer'=1,'inner'=32] {'outer','inner'}, use_global_device_ids=true, to_apply=%region_3.0 | all-reduce | flops 4096 | bytes 32768 | tf_op jit(solution)/shard_map/psum | solution.py:88
  620.7 5.8 cholesky.17
  626.6 0.6 compare_reduce_fusion
  627.2 0.7 fusion.13
  627.9 4.9 custom-call.6
  633.3 0.8 fusion.27
  634.0 0.8 fusion.28
  634.8 0.6 gather_fusion
  635.4 0.7 convolution_bitcast_fusion.1
  636.4 0.7 convolution_bitcast_fusion
  637.3 40.4 %all-reduce.1 = (f32[64,64]{0,1:T(8,128)S(1)}, f32[64,64]{0,1:T(8,128)S(1)}) all-reduce(f32[64,64]{0,1:T(8,128)S(1)} %convolution_bitcast_fusion.5, f32[64,64]{0,1:T(8,128)S(1)} %convolution_bitcast_fusion.4), channel_id=1, replica_groups=mesh['outer'=1,'inner'=32] {'outer','inner'}, use_global_device_ids=true, to_apply=%region_6.7 | all-reduce | flops 8192 | bytes 65536 | tf_op jit(solution)/shard_map/psum | solution.py:107
  677.7 0.7 copy.69
  678.4 0.7 copy.70
  (73 shorter events, 6.0 us)
Async XLA Ops:
  7.2 628.2 %copy-start = (f32[1024,128]{1,0:T(8,128)S(1)}, f32[1024,128]{1,0:T(8,128)}, u32[]{:S(2)}) copy-start(f32[1024,128]{1,0:T(8,128)} %param.37) | copy-start | bytes 1572868
  7.2 1.5 copy-start.6
  7.2 134.1 %all-reduce.10.cloned.1.call-start = ((), (), s32[]{:S(2)}) async-start(), calls=%async_computation.2 | async-start | bytes 262144
  9.0 0.7 copy-start.16
  10.8 288.5 %all-reduce.6.cloned.1.call-start = ((), (), s32[]{:S(2)}) async-start(), calls=%async_computation | async-start | bytes 131072 | tf_op jit(solution)/shard_map/psum | solution.py:57
  10.8 130.5 %copy-start.17 = (f32[8,64]{1,0:T(8,128)S(1)}, f32[8,64]{1,0:T(8,128)}, u32[]{:S(2)}) copy-start(f32[8,64]{1,0:T(8,128)} %param.21) | copy-start | bytes 6148
  142.0 40.0 %copy-start.10 = (f32[8,256]{1,0:T(8,128)S(1)}, f32[8,256]{1,0:T(8,128)}, u32[]{:S(2)}) copy-start(f32[8,256]{1,0:T(8,128)} %param.28) | copy-start | bytes 24580
  182.0 0.7 copy-start.11
  183.6 0.7 copy-start.19
  183.6 0.7 copy-start.18
  183.6 394.9 %all-reduce.8.cloned.1.call-start = ((), (), s32[]{:S(2)}) async-start(), calls=%async_computation.1 | async-start | bytes 262144 | tf_op jit(solution)/shard_map/psum | solution.py:79
  221.3 78.0 %copy-start.12 = (f32[8,256]{1,0:T(8,128)S(1)}, f32[8,256]{1,0:T(8,128)}, u32[]{:S(2)}) copy-start(f32[8,256]{1,0:T(8,128)} %param.32) | copy-start | bytes 24580
  300.2 40.4 %copy-start.13 = (f32[8,256]{1,0:T(8,128)S(1)}, f32[8,256]{1,0:T(8,128)}, u32[]{:S(2)}) copy-start(f32[8,256]{1,0:T(8,128)} %param.33) | copy-start | bytes 24580
  340.8 37.0 %copy-start.14 = (f32[8,256]{1,0:T(8,128)S(1)}, f32[8,256]{1,0:T(8,128)}, u32[]{:S(2)}) copy-start(f32[8,256]{1,0:T(8,128)} %param.31) | copy-start | bytes 24580
  377.9 38.3 %copy-start.15 = (f32[8,256]{1,0:T(8,128)S(1)}, f32[8,256]{1,0:T(8,128)}, u32[]{:S(2)}) copy-start(f32[8,256]{1,0:T(8,128)} %param.29) | copy-start | bytes 24580
  416.4 37.3 %copy-start.9 = (f32[8,512]{1,0:T(8,128)S(1)}, f32[8,512]{1,0:T(8,128)}, u32[]{:S(2)}) copy-start(f32[8,512]{1,0:T(8,128)} %param.36) | copy-start | bytes 49156
  453.4 0.7 copy-start.8
  453.4 1.0 copy-start.5
  453.8 1.1 copy-start.7
  454.1 1.1 copy-start.1
  579.4 0.8 copy-start.2
  633.2 3.8 copy-start.3
  635.4 1.0 copy-start.4
Sparse Core Ops, SparseCore 0:
  14.1 127.1 all-reduce.9
  183.7 115.4 all-reduce.5
  456.5 121.9 all-reduce.7
where the time goes:
time: 686 us
  waiting for transfers between devices  330 us (48%)
  blocking collectives  309 us (45%)
  between operations  14.1 us (2%)
  other arithmetic  13.7 us (2%)
  matrix products  13.6 us (2%)
    unnamed x4, waiting for transfers between devices  130 us
    psum x1, waiting for transfers between devices, shards(): coefficients = lax.psum(projected, ('outer', 'inner')) / node_count  122 us
    psum x1, waiting for transfers between devices, shards(): summed = lax.psum(matmul_exact(sep_lower, y_sep), ('outer', 'inner'))  77.8 us
    psum x1, blocking collectives, shards(): g_summed, c_summed = lax.psum((g_local, c_local), ('outer', 'inner'))  40.4 us
    all_gather x1, blocking collectives, shards(): y_root_all = lax.all_gather(y_root, ('outer', 'inner'), axis=0, tiled=True)  40.4 us
    all_gather x1, blocking collectives, shards(): sep_whole = lax.all_gather(b_sep - t_sep, 'inner', axis=0, tiled=True)  40 us
    psum x1, blocking collectives, shards(): gram_matrix = lax.psum(local_gram, ('outer', 'inner')) / node_count  39.4 us
    all_gather x1, blocking collectives, shards(): z_sep_all = lax.all_gather(z_sep, 'inner', axis=0, tiled=True)  38.3 us
  transfers between devices with their start and end apart: 3, of which 3 were waited for; matrix products, arithmetic and copies ran while one was open for 0% of the time, Pallas kernels for 0%

commit v1 on v0

--- a/solution.py
+++ b/solution.py
@@ -76,7 +76,8 @@
         + contract_rows(basis_sep, x_sep)
         + contract_rows(basis_root, x_root)
     )
-    coefficients = lax.psum(projected, ("outer", "inner")) / node_count
+    expand_the_positions = lambda chunk, ax_name: jnp.sum(lax.all_gather(chunk, ax_name), 0)
+    coefficients = expand_the_positions(projected, ("outer", "inner")) / node_count
     cleaned = [
         values - matmul_exact(basis, coefficients) for basis, values in zip(pieces_q, pieces_x)
     ]

time: 686 us -> 635 us (0.926)
  waiting for transfers between devices: 330 us -> 267 us
  matrix products: 13.6 us -> 22.7 us
    psum x1 -> x0, waiting for transfers between devices: 122 us -> none  [shards(): coefficients = lax.psum(projected, ('outer', 'inner')) / node_count]
    all_gather x0 -> x1, waiting for transfers between devices: none -> 59.2 us  [shards(): lax.all_gather(chunk, ax_name)]
    dot_general x17, matrix products: 8.18 us -> 15.2 us  [matmul_exact(): jnp.dot(left, right, precision=lax.Precision.HIGHEST, preferred_element_t...]
where the time goes in v1:
time: 635 us; the launch traced here: 634 us
  blocking collectives  310 us (49%)
  waiting for transfers between devices  267 us (42%)
  matrix products  22.7 us (4%)
  between operations  14 us (2%)
  other arithmetic  13.5 us (2%)
  local copies, waits for them, and re-layouts  6.81 us (1%)
    unnamed x4, waiting for transfers between devices  130 us
    psum x1, waiting for transfers between devices, shards(): summed = lax.psum(matmul_exact(sep_lower, y_sep), ('outer', 'inner'))  78.2 us
    all_gather x1, waiting for transfers between devices, shards(): lax.all_gather(chunk, ax_name)  59.2 us
    psum x1, blocking collectives, shards(): g_summed, c_summed = lax.psum((g_local, c_local), ('outer', 'inner'))  40.4 us
    all_gather x1, blocking collectives, shards(): y_root_all = lax.all_gather(y_root, ('outer', 'inner'), axis=0, tiled=True)  40.2 us
    all_gather x1, blocking collectives, shards(): sep_whole = lax.all_gather(b_sep - t_sep, 'inner', axis=0, tiled=True)  39.9 us
    psum x1, blocking collectives, shards(): gram_matrix = lax.psum(local_gram, ('outer', 'inner')) / node_count  39.6 us
    all_gather x1, blocking collectives, shards(): z_sep_all = lax.all_gather(z_sep, 'inner', axis=0, tiled=True)  38.3 us
  transfers between devices with their start and end apart: 3, of which 3 were waited for; matrix products, arithmetic and copies ran while one was open for 0% of the time, Pallas kernels for 0%

profile of v1, /device:TPU:0, one launch (start us, length us, event | category | flops | bytes accessed | tf_op | source)
XLA Modules:
  0.0 633.8 jit_solution(4248371004321635002)
XLA Ops:
  7.2 1.4 fusion.17
  8.6 1.3 fusion.18
  10.0 1.7 fusion.8
  11.8 129.5 %all-reduce.7.cloned.1.call-done = f32[256,64]{1,0:T(8,128)} async-done(((f32[256,64]{1,0:T(8,128)}), f32[256,64]{1,0:T(8,128)}) %all-reduce.7.cloned.1.call-update) | async-done | bytes 65552
  141.3 0.7 dynamic-slice_subtract_fusion
  142.0 39.9 %all_gather.24 = f32[256,64]{1,0:T(8,128)S(1)} all-gather(f32[8,64]{1,0:T(8,128)S(1)} %dynamic-slice_subtract_fusion), channel_id=1, replica_groups=mesh['outer'=1,'inner'=32] {'inner'}, dimensions={0}, use_global_device_ids=true | all-gather | bytes 67584 | tf_op jit(solution)/shard_map/all_gather | solution.py:55
  181.9 0.9 fusion.19
  182.8 1.6 convolution_bitcast_fusion.3
  184.4 37.2 %all_gather.25 = f32[256,64]{1,0:T(8,128)S(1)} all-gather(f32[8,64]{1,0:T(8,128)} %param.22), channel_id=1, replica_groups=mesh['outer'=1,'inner'=32] {'outer','inner'}, dimensions={0}, use_global_device_ids=true | all-gather | bytes 67584 | tf_op jit(solution)/shard_map/all_gather | solution.py:58
  221.8 78.2 %all-reduce.5.cloned.1.call-done = f32[256,64]{0,1:T(8,128)} async-done(((f32[256,64]{0,1:T(8,128)}), f32[256,64]{0,1:T(8,128)}) %all-reduce.5.cloned.1.call-update) | async-done | bytes 65552 | tf_op jit(solution)/shard_map/psum | solution.py:57
  300.0 1.0 convolution_bitcast_fusion.8
  301.0 40.2 %all_gather.26 = f32[256,64]{1,0:T(8,128)S(1)} all-gather(f32[8,64]{1,0:T(8,128)S(1)} %convolution_bitcast_fusion.8), channel_id=1, replica_groups=mesh['outer'=1,'inner'=32] {'outer','inner'}, dimensions={0}, use_global_device_ids=true | all-gather | bytes 67584 | tf_op jit(solution)/shard_map/all_gather | solution.py:60
  341.2 0.9 fusion.20
  342.1 37.0 %all_gather.27 = f32[256,64]{1,0:T(8,128)S(1)} all-gather(f32[8,64]{1,0:T(8,128)S(1)} %bitcast.125), channel_id=1, replica_groups=mesh['outer'=1,'inner'=32] {'outer','inner'}, dimensions={0}, use_global_device_ids=true | all-gather | bytes 67584 | tf_op jit(solution)/shard_map/all_gather | solution.py:62
  379.0 0.9 fusion.5
  379.9 38.3 %all_gather.28 = f32[256,64]{1,0:T(8,128)S(1)} all-gather(f32[8,64]{1,0:T(8,128)S(1)} %fusion.5), channel_id=1, replica_groups=mesh['outer'=1,'inner'=32] {'inner'}, dimensions={0}, use_global_device_ids=true | all-gather | bytes 67584 | tf_op jit(solution)/shard_map/all_gather | solution.py:64
  418.2 0.9 fusion.21
  419.1 37.0 %all_gather.29 = f32[256,64]{1,0:T(8,128)S(1)} all-gather(f32[8,64]{1,0:T(8,128)S(1)} %bitcast.126), channel_id=1, replica_groups=mesh['outer'=1,'inner'=32] {'inner'}, dimensions={0}, use_global_device_ids=true | all-gather | bytes 67584 | tf_op jit(solution)/shard_map/all_gather | solution.py:66
  456.1 1.0 fusion.6
  457.1 1.0 fusion.23
  458.2 1.0 fusion.24
  459.2 1.3 fusion.2
  460.5 1.3 fusion.22
  461.9 1.1 fusion.1
  463.1 59.2 %all-gather.3.cloned.1.call-done = f32[16384,64]{0,1:T(8,128)} async-done(((f32[512,64]{0,1:T(8,128)}), f32[16384,64]{0,1:T(8,128)}) %all-gather.3.cloned.1.call-update) | async-done | bytes 4194320 | tf_op jit(solution)/shard_map/all_gather | solution.py:79
  522.3 4.6 copy.81
  529.4 39.6 %psum.29 = f32[64,64]{0,1:T(8,128)S(1)} all-reduce(f32[64,64]{0,1:T(8,128)S(1)} %convolution_add_fusion.1), channel_id=1, replica_groups=mesh['outer'=1,'inner'=32] {'outer','inner'}, use_global_device_ids=true, to_apply=%region_3.0 | all-reduce | flops 4096 | bytes 32768 | tf_op jit(solution)/shard_map/psum | solution.py:89
  569.1 5.8 cholesky.17
  576.3 4.9 custom-call.6
  581.6 0.8 fusion.28
  582.4 0.8 fusion.27
  585.5 40.4 %all-reduce.1 = (f32[64,64]{0,1:T(8,128)S(1)}, f32[64,64]{0,1:T(8,128)S(1)}) all-reduce(f32[64,64]{0,1:T(8,128)S(1)} %convolution_bitcast_fusion.5, f32[64,64]{0,1:T(8,128)S(1)} %convolution_bitcast_fusion.4), channel_id=1, replica_groups=mesh['outer'=1,'inner'=32] {'outer','inner'}, use_global_device_ids=true, to_apply=%region_6.7 | all-reduce | flops 8192 | bytes 65536 | tf_op jit(solution)/shard_map/psum | solution.py:108
  (51 shorter events, 8.4 us)
Async XLA Ops:
  7.2 576.6 %copy-start = (f32[1024,128]{1,0:T(8,128)S(1)}, f32[1024,128]{1,0:T(8,128)}, u32[]{:S(2)}) copy-start(f32[1024,128]{1,0:T(8,128)} %param.38) | copy-start | bytes 1572868
  7.2 454.7 %copy-start.1 = (f32[256,512]{1,0:T(8,128)S(1)}, f32[256,512]{1,0:T(8,128)}, u32[]{:S(2)}) copy-start(f32[256,512]{1,0:T(8,128)} %param.34) | copy-start | bytes 1572868
  7.2 455.8 %copy-start.7 = (s32[2,4]{1,0:T(2,128)S(1)}, s32[2,4]{1,0:T(2,128)}, u32[]{:S(2)}) copy-start(s32[2,4]{1,0:T(2,128)} %param.39) | copy-start | bytes 100
  7.2 134.1 %all-reduce.7.cloned.1.call-start = ((), (), s32[]{:S(2)}) async-start(), calls=%async_computation.2 | async-start | bytes 262144
  11.7 288.3 %all-reduce.5.cloned.1.call-start = ((), (), s32[]{:S(2)}) async-start(), calls=%async_computation | async-start | bytes 131072 | tf_op jit(solution)/shard_map/psum | solution.py:57
  184.4 337.9 %all-gather.3.cloned.1.call-start = ((), (), s32[]{:S(2)}) async-start(), calls=%async_computation.1 | async-start | bytes 4325376 | tf_op jit(solution)/shard_map/all_gather | solution.py:79
  526.8 1.4 copy-start.5
  526.9 1.5 copy-start.6
  526.9 57.7 %copy-start.4 = (f32[1024,128]{1,0:T(8,128)S(1)}, f32[1024,128]{1,0:T(8,128)}, u32[]{:S(2)}) copy-start(f32[1024,128]{1,0:T(8,128)} %param.37) | copy-start | bytes 1572868
  527.6 99.7 %copy-start.2 = (f32[512,64]{0,1:T(8,128)}, f32[512,64]{0,1:T(8,128)S(1)}, u32[]{:S(2)}) copy-start(f32[512,64]{0,1:T(8,128)S(1)} %broadcast_multiply_fusion) | copy-start | bytes 393220
  581.6 45.7 %copy-start.3 = (f32[256,64]{0,1:T(8,128)}, f32[256,64]{0,1:T(8,128)S(1)}, u32[]{:S(2)}) copy-start(f32[256,64]{0,1:T(8,128)S(1)} %fusion.26) | copy-start | bytes 196612
Sparse Core Ops, SparseCore 0:
  14.1 127.1 all-reduce.6
  184.5 115.4 all-reduce.4
  463.1 59.1 all-gather.2
